TPU v7x, 512 devices: a whole 4x4x16 slice. The times are simulated.
512 devices in a mesh: region: 16 (over z), slab: 32 (over x, y, core).
Axes of the slice: x: 4, y: 4, z: 16, core: 2. Of those that a mesh axis runs over, the one named last changes fastest.
Arguments:
- records: bfloat16 [16384, 4096], P('region', 'slab'), may hold values from -6 to 6
- first_station: int32 [65536], P(('region', 'slab')), may hold values from 0 to 1023
- second_region: int32 [65536, 1], P(('region', 'slab')), may hold values from 0 to 15; in each aligned block of 128 rows (0 to 127, 128 to 255, ...) at most 16 rows name the same one
- second_station: int32 [65536], P(('region', 'slab')), may hold values from 0 to 1023
Outputs:
- stacks: bfloat16 [65536, 2048], P(('region', 'slab'))
Inputs may be any that keep to these rules, and one draw needn't show every extreme that they name: `second_region`: no region is named by more than 16 pairs of one device.
All inputs are finite; a program needn't handle non-finite values.
Results may differ from a plain program's by a relative error of at most 0.0077.
Values may be sent and summed in bfloat16 or wider, within the bound.
A program may use at most 64 MiB of HBM per device.

v0:
```python
import math
import jax
import jax.numpy as jnp
from jax import lax
from jax.sharding import PartitionSpec as P

NFFT = 2048
BINS = 1024
SEG = 2
HALF = 4


def dft_table():
    sample = jnp.arange(NFFT, dtype=jnp.int32)[:, None]
    frequency = jnp.arange(BINS, dtype=jnp.int32)[None, :]
    phase = (sample * frequency % NFFT).astype(jnp.float32) * (2.0 * math.pi / NFFT)
    return jnp.concatenate([jnp.cos(phase), -jnp.sin(phase)], axis=1).astype(jnp.bfloat16)


def whitened(traces):
    count = traces.shape[0]
    signal = traces.astype(jnp.float32).reshape(count * SEG, NFFT)
    signal = signal - jnp.mean(signal, axis=1, keepdims=True)
    position = jnp.arange(NFFT, dtype=jnp.int32).astype(jnp.float32)
    taper = 0.5 - 0.5 * jnp.cos(position * (2.0 * math.pi / NFFT))
    tapered = (signal * taper[None, :]).astype(jnp.bfloat16)
    spectrum = jnp.dot(tapered, dft_table(), preferred_element_type=jnp.float32)
    real_part = spectrum[:, :BINS]
    imag_part = spectrum[:, BINS:]
    amplitude = jnp.sqrt(real_part * real_part + imag_part * imag_part + 1e-06)
    padded = jnp.pad(amplitude, ((0, 0), (HALF, HALF)))
    smooth = jnp.zeros_like(amplitude)
    for offset in range(2 * HALF + 1):
        smooth = smooth + padded[:, offset : offset + BINS]
    smooth = smooth / (2 * HALF + 1)
    level = jnp.mean(amplitude, axis=1, keepdims=True)
    divisor = smooth + level + 1e-06
    white = spectrum / jnp.concatenate([divisor, divisor], axis=1)
    return white.astype(jnp.bfloat16).reshape(count, SEG * NFFT)


def cross(first_rows, second_rows):
    left = first_rows.astype(jnp.float32).reshape(first_rows.shape[:-1] + (SEG, 2, BINS))
    right = second_rows.astype(jnp.float32).reshape(second_rows.shape[:-1] + (SEG, 2, BINS))
    real_sum = jnp.mean(
        left[..., 0, :] * right[..., 0, :] + left[..., 1, :] * right[..., 1, :], axis=-2
    )
    imag_sum = jnp.mean(
        left[..., 0, :] * right[..., 1, :] - left[..., 1, :] * right[..., 0, :], axis=-2
    )
    return jnp.concatenate([real_sum, imag_sum], axis=-1).astype(jnp.bfloat16)


def local(records, first_station, second_region, second_station):
    regions = lax.axis_size("region")
    pair_count = first_station.shape[0]
    capacity = max(2, pair_count // regions + pair_count // 16)
    arrived = lax.all_to_all(records, "slab", split_axis=0, concat_axis=1, tiled=True)
    spectra = whitened(arrived)
    width = spectra.shape[1]
    target = second_region[:, 0]
    onehot = (target[:, None] == jnp.arange(regions, dtype=jnp.int32)[None, :]).astype(jnp.int32)
    ranking = jnp.sum((jnp.cumsum(onehot, axis=0) - onehot) * onehot, axis=1)
    slot_index = target * capacity + ranking
    requests = (
        jnp.zeros((regions * capacity,), jnp.int32)
        .at[slot_index]
        .set(second_station)
        .reshape(regions, capacity)
    )
    incoming = lax.all_to_all(requests, "region", split_axis=0, concat_axis=0, tiled=True)
    wanted = jnp.concatenate([first_station, incoming.reshape(-1)])
    initial = jnp.zeros((wanted.shape[0], width), jnp.bfloat16)
    piece = lax.all_gather(spectra, "slab", axis=0, tiled=True)
    inside = (wanted >= 0) & (wanted < piece.shape[0])
    chosen = jnp.take(piece, jnp.clip(wanted, 0, piece.shape[0] - 1), axis=0)
    picked = jnp.where(inside[:, None], chosen, initial)
    first_rows = picked[:pair_count]
    served = picked[pair_count:]
    returned = lax.all_to_all(
        served.reshape(regions, capacity, width), "region", split_axis=0, concat_axis=0, tiled=True
    )
    second_rows = jnp.take(returned.reshape(regions * capacity, width), slot_index, axis=0)
    stacks = cross(first_rows, second_rows)
    return stacks


def solution(mesh):
    placed = (
        P("region", "slab"),
        P(("region", "slab")),
        P(("region", "slab"), None),
        P(("region", "slab")),
    )
    return jax.shard_map(
        local, mesh=mesh, in_specs=placed, out_specs=P(("region", "slab"), None), check_vma=False
    )
```

profile of v0, /device:TPU:32, one launch (start us, length us, event | category | flops | bytes accessed | tf_op | source)
XLA Modules:
  0.0 269.8 jit_solution(3383094113395302440)
XLA Ops:
  6.5 7.3 %all-to-all-start.1 = ((bf16[32,32,128]{2,1,0:T(8,128)(2,1)}), bf16[32,32,128]{2,1,0:T(8,128)(2,1)S(1)}, u32[]{:S(2)}, u32[]{:S(2)}) async-start(bf16[32,32,128]{2,1,0:T(8,128)(2,1)} %bitcast.20), calls=%async_computation.1 | async-start | bytes 524288 | tf_op jit(solution)/shard_map/all_to_all | solution.py:58
  13.9 0.0 all-gather.2.cloned.1.call-start
  13.9 34.9 %negate_convert_fusion = (bf16[2048,1024]{1,0:T(8,128)(2,1)}, bf16[2048,1024]{1,0:T(8,128)(2,1)}) fusion(), kind=kLoop, calls=%fused_computation.13 | loop fusion | flops 35651584 | bytes 8388608 | tf_op jit(solution)/shard_map/convert.6
  48.9 0.1 multiply_subtract_fusion
  48.9 0.0 all-to-all-done.1
  48.9 0.2 convert_reduce_fusion
  49.1 0.1 copy.8
  49.2 0.1 reduce_sum.60
  49.3 0.1 reduce_sum.61
  49.4 0.1 convert_bitcast_fusion
  49.5 0.3 copy.7
  49.8 0.1 reshape.149
  49.9 0.0 copy-start.2
  49.9 0.0 copy-start.3
  49.9 4.4 %fusion.3 = f32[64,2048]{1,0:T(8,128)S(1)} fusion(bf16[2048,1024]{1,0:T(8,128)(2,1)} %get-tuple-element.13, bf16[2048,1024]{1,0:T(8,128)(2,1)} %get-tuple-element.14, f32[64,2048]{1,0:T(8,128)S(1)} %reshape.149, f32[2048]{0:T(1024)S(1)} %multiply_subtract_fusion, f32[64]{0:T(128)S(1)} %broadcast_multiply_fusion.1), kind=kOutput, calls=%fused_computation.9 | convolution fusion | flops 554041344 | bytes 9445632 | tf_op jit(solution)/shard_map/dot_general | solution.py:27
  54.3 0.2 fusion.33
  54.5 0.6 fusion.22
  55.2 0.1 fusion.11
  55.2 0.8 reshape.144
  56.0 0.0 all-gather.2.cloned.1.call-update
  56.0 0.0 copy-done.2
  56.0 0.1 fusion.28
  56.1 0.2 reduce_window_sum.11
  56.3 0.2 select_reduce_fusion
  56.5 1.1 scatter_custom_fusion
  57.6 0.7 all_to_all.19
  58.3 15.2 %all-to-all-start = ((s32[16,1,16]{2,1,0:T(1,128)}), s32[16,1,16]{2,1,0:T(1,128)S(1)}, u32[]{:S(2)}, u32[]{:S(2)}) async-start(s32[16,1,16]{2,1,0:T(1,128)} %all_to_all.19), calls=%async_computation | async-start | bytes 16384 | tf_op jit(solution)/shard_map/all_to_all | solution.py:71
  73.5 0.0 copy-done.3
  73.5 11.0 %all-to-all-done = s32[16,1,16]{2,1,0:T(1,128)S(1)} async-done(((s32[16,1,16]{2,1,0:T(1,128)}), s32[16,1,16]{2,1,0:T(1,128)S(1)}, u32[]{:S(2)}, u32[]{:S(2)}) %all-to-all-start) | async-done | bytes 1056 | tf_op jit(solution)/shard_map/all_to_all | solution.py:71
  84.6 0.1 concatenate.43
  84.6 0.5 broadcast.142
  85.1 0.6 reduce.12
  85.7 0.1 concatenate.38
  85.9 42.7 %all-gather.2.cloned.1.call-done = bf16[1024,4096]{1,0:T(8,128)(2,1)} async-done(((bf16[32,4096]{1,0:T(8,128)(2,1)}), bf16[1024,4096]{1,0:T(8,128)(2,1)}) %all-gather.2.cloned.1.call-update) | async-done | bytes 8388624 | tf_op jit(solution)/shard_map/all_gather | solution.py:74
  128.6 12.0 %gather_fusion = bf16[384,4096]{1,0:T(8,128)(2,1)S(1)} fusion(bf16[1024,4096]{1,0:T(8,128)(2,1)} %all-gather.2.cloned.1.call-done, s32[1024]{0:T(1024)S(1)} %pad_clamp_fusion.1), kind=kCustom, calls=%fused_computation | custom fusion | bytes 6292992 | tf_op jit(solution)/shard_map/jit(_take)/gather | solution.py:76
  140.5 0.5 select_select_fusion
  141.0 1.7 copy-done
  142.7 1.5 slice.77
  144.2 12.7 %all-to-all-start.2 = ((bf16[16,16,4096]{2,1,0:T(8,128)(2,1)}), bf16[16,16,4096]{2,1,0:T(8,128)(2,1)S(1)}, u32[]{:S(2)}, u32[]{:S(2)}) async-start(bf16[16,16,4096]{2,1,0:T(8,128)(2,1)} %bitcast.19), calls=%async_computation.2 | async-start | bytes 4194304 | tf_op jit(solution)/shard_map/all_to_all | solution.py:80
  156.9 2.8 %slice_convert_fusion = f32[128,4096]{1,0:T(8,128)} fusion(bf16[384,4096]{1,0:T(8,128)(2,1)} %copy-done), kind=kLoop, calls=%fused_computation.21 | loop fusion | flops 524288 | bytes 3145728 | tf_op jit(solution)/shard_map/reshape | solution.py:43
  159.7 4.0 %reshape.151 = f32[128,2,2,1024]{3,2,1,0:T(2,128)} reshape(f32[128,4096]{1,0:T(8,128)} %slice_convert_fusion) | data formatting | bytes 4194304 | tf_op jit(solution)/shard_map/reshape | solution.py:43
  163.7 87.5 %all-to-all-done.2 = bf16[16,16,4096]{2,1,0:T(8,128)(2,1)S(1)} async-done(((bf16[16,16,4096]{2,1,0:T(8,128)(2,1)}), bf16[16,16,4096]{2,1,0:T(8,128)(2,1)S(1)}, u32[]{:S(2)}, u32[]{:S(2)}) %all-to-all-start.2) | async-done | bytes 2097184 | tf_op jit(solution)/shard_map/all_to_all | solution.py:80
  251.2 1.2 gather_fusion.1
  252.4 0.0 copy-start.1
  252.4 1.6 gather.12
  254.0 2.2 fusion.10
  256.2 5.8 %add_reduce_fusion = (f32[128,1024]{1,0:T(8,128)S(1)}, f32[128,1024]{1,0:T(8,128)S(1)}) fusion(f32[128,2,2,1024]{3,2,1,0:T(2,128)S(1)} %fusion.10, f32[128,2,2,1024]{3,2,1,0:T(2,128)S(1)} %copy-done.1), kind=kLoop, calls=%fused_computation.23 | loop fusion | flops 1835008 | bytes 5242880 | tf_op jit(solution)/shard_map/reduce_sum | solution.py:45
  262.1 0.8 pad_maximum_fusion
  (14 shorter events, 0.2 us)
Async XLA Ops:
  6.5 42.4 %all-to-all-start.1 = ((bf16[32,32,128]{2,1,0:T(8,128)(2,1)}), bf16[32,32,128]{2,1,0:T(8,128)(2,1)S(1)}, u32[]{:S(2)}, u32[]{:S(2)}) async-start(bf16[32,32,128]{2,1,0:T(8,128)(2,1)} %bitcast.20), calls=%async_computation.1 | async-start | bytes 524288 | tf_op jit(solution)/shard_map/all_to_all | solution.py:58
  13.9 114.7 %all-gather.2.cloned.1.call-start = ((), (), s32[]{:S(2)}) async-start(), calls=%async_computation.3 | async-start | bytes 8650752 | tf_op jit(solution)/shard_map/all_gather | solution.py:74
  49.9 6.2 %copy-start.2 = (s32[128,1]{0,1:T(1,128)S(1)}, s32[128,1]{0,1:T(1,128)}, u32[]{:S(2)}) copy-start(s32[128,1]{0,1:T(1,128)} %param.6) | copy-start | bytes 1540
  49.9 23.6 %copy-start.3 = (s32[128]{0:T(128)S(1)}, s32[128]{0:T(128)}, u32[]{:S(2)}) copy-start(s32[128]{0:T(128)} %param.5) | copy-start | bytes 1540
  58.3 26.3 %all-to-all-start = ((s32[16,1,16]{2,1,0:T(1,128)}), s32[16,1,16]{2,1,0:T(1,128)S(1)}, u32[]{:S(2)}, u32[]{:S(2)}) async-start(s32[16,1,16]{2,1,0:T(1,128)} %all_to_all.19), calls=%async_computation | async-start | bytes 16384 | tf_op jit(solution)/shard_map/all_to_all | solution.py:71
  141.0 1.7 copy-start
  144.2 107.0 %all-to-all-start.2 = ((bf16[16,16,4096]{2,1,0:T(8,128)(2,1)}), bf16[16,16,4096]{2,1,0:T(8,128)(2,1)S(1)}, u32[]{:S(2)}, u32[]{:S(2)}) async-start(bf16[16,16,4096]{2,1,0:T(8,128)(2,1)} %bitcast.19), calls=%async_computation.2 | async-start | bytes 4194304 | tf_op jit(solution)/shard_map/all_to_all | solution.py:80
  252.4 3.8 %copy-start.1 = (f32[128,2,2,1024]{3,2,1,0:T(2,128)S(1)}, f32[128,2,2,1024]{3,2,1,0:T(2,128)}, u32[]{:S(2)}) copy-start(f32[128,2,2,1024]{3,2,1,0:T(2,128)} %reshape.151) | copy-start | bytes 6291460
Sparse Core Ops, SparseCore 0:
  56.2 72.3 all-gather.1
where the time goes:
time: 270 us
  waiting for transfers between devices  141 us (52%)
  other arithmetic  49.5 us (18%)
  starting transfers between devices  35.2 us (13%)
  local copies, waits for them, and re-layouts  25.8 us (10%)
  between operations  13.6 us (5%)
  matrix products  4.41 us (2%)
    all_to_all x1, waiting for transfers between devices, local(): lax.all_to_all(served.reshape(regions, capacity, width), 'region', split_...  87.5 us
    all_gather x1, waiting for transfers between devices, local(): piece = lax.all_gather(spectra, 'slab', axis=0, tiled=True)  42.7 us
    another operation x3, other arithmetic  35 us
    all_to_all x1, starting transfers between devices, local(): lax.all_to_all(requests, 'region', split_axis=0, concat_axis=0, tiled=True)  15.2 us
    all_to_all x1, starting transfers between devices, local(): lax.all_to_all(served.reshape(regions, capacity, width), 'region', split_...  12.7 us
    gather x1, local copies, waits for them, and re-layouts, local(): chosen = jnp.take(piece, jnp.clip(wanted, 0, piece.shape[0] - 1), axis=0)  12 us
    all_to_all x1, waiting for transfers between devices, local(): lax.all_to_all(requests, 'region', split_axis=0, concat_axis=0, tiled=True)  11 us
    all_to_all x1, starting transfers between devices, local(): lax.all_to_all(records, 'slab', split_axis=0, concat_axis=1, tiled=True)  7.32 us
  transfers between devices with their start and end apart: 4, of which 3 were waited for; matrix products, arithmetic and copies ran while one was open for 17% of the time, Pallas kernels for 0%

commit v1 on v0

--- a/solution.py
+++ b/solution.py
@@ -55,7 +55,10 @@
     regions = lax.axis_size("region")
     pair_count = first_station.shape[0]
     capacity = max(2, pair_count // regions + pair_count // 16)
-    arrived = lax.all_to_all(records, "slab", split_axis=0, concat_axis=1, tiled=True)
+    arrived = jnp.concatenate(
+        lax.all_to_all(jnp.stack(jnp.split(records, lax.axis_size("slab"), axis=0)), "slab", 0, 0),
+        axis=1,
+    )
     spectra = whitened(arrived)
     width = spectra.shape[1]
     target = second_region[:, 0]

time: 270 us -> 313 us (1.16)
  local copies, waits for them, and re-layouts: 25.8 us -> 67.2 us
    unnamed x9 -> x40, local copies, waits for them, and re-layouts: 1.69 us -> 41.8 us
  transfers between devices with their start and end apart: 4 -> 4, of which waited for: 3 -> 3; matrix products, arithmetic and copies ran while one was open for 17% -> 14% of each run, Pallas kernels for 0% -> 0%
where the time goes in v1:
time: 313 us; the launch traced here: 311 us
  waiting for transfers between devices  141 us (45%)
  local copies, waits for them, and re-layouts  67.2 us (21%)
  other arithmetic  49.5 us (16%)
  starting transfers between devices  35.2 us (11%)
  between operations  13.7 us (4%)
  matrix products  4.41 us (1%)
    all_to_all x1, waiting for transfers between devices, local(): lax.all_to_all(served.reshape(regions, capacity, width), 'region', split_...  87.5 us
    all_gather x1, waiting for transfers between devices, local(): piece = lax.all_gather(spectra, 'slab', axis=0, tiled=True)  42.7 us
    unnamed x40, local copies, waits for them, and re-layouts  41.8 us
    another operation x3, other arithmetic  35 us
    all_to_all x1, starting transfers between devices, local(): lax.all_to_all(requests, 'region', split_axis=0, concat_axis=0, tiled=True)  15.2 us
    all_to_all x1, starting transfers between devices, local(): lax.all_to_all(served.reshape(regions, capacity, width), 'region', split_...  12.7 us
    gather x1, local copies, waits for them, and re-layouts, local(): chosen = jnp.take(piece, jnp.clip(wanted, 0, piece.shape[0] - 1), axis=0)  12 us
    all_to_all x1, waiting for transfers between devices, local(): lax.all_to_all(requests, 'region', split_axis=0, concat_axis=0, tiled=True)  11 us
  transfers between devices with their start and end apart: 4, of which 3 were waited for; matrix products, arithmetic and copies ran while one was open for 14% of the time, Pallas kernels for 0%

profile of v1, /device:TPU:32, one launch (start us, length us, event | category | flops | bytes accessed | tf_op | source)
XLA Modules:
  0.0 311.2 jit_solution(10122652128425730091)
XLA Ops:
  6.5 1.3 constant_dynamic-update-slice_fusion.32
  7.8 1.3 constant_dynamic-update-slice_fusion.31
  9.1 1.3 constant_dynamic-update-slice_fusion.30
  10.4 1.3 constant_dynamic-update-slice_fusion.29
  11.7 1.3 constant_dynamic-update-slice_fusion.28
  13.0 1.3 constant_dynamic-update-slice_fusion.27
  14.3 1.3 constant_dynamic-update-slice_fusion.26
  15.6 1.3 constant_dynamic-update-slice_fusion.25
  16.9 1.3 constant_dynamic-update-slice_fusion.24
  18.2 1.3 constant_dynamic-update-slice_fusion.23
  19.5 1.3 constant_dynamic-update-slice_fusion.22
  20.8 1.3 constant_dynamic-update-slice_fusion.21
  22.1 1.3 constant_dynamic-update-slice_fusion.20
  23.4 1.3 constant_dynamic-update-slice_fusion.19
  24.7 1.3 constant_dynamic-update-slice_fusion.18
  26.0 1.3 constant_dynamic-update-slice_fusion.17
  27.3 1.3 constant_dynamic-update-slice_fusion.16
  28.6 1.3 constant_dynamic-update-slice_fusion.15
  29.8 1.3 constant_dynamic-update-slice_fusion.14
  31.1 1.3 constant_dynamic-update-slice_fusion.13
  32.4 1.3 constant_dynamic-update-slice_fusion.12
  33.7 1.3 constant_dynamic-update-slice_fusion.11
  35.0 1.3 constant_dynamic-update-slice_fusion.10
  36.3 1.3 constant_dynamic-update-slice_fusion.9
  37.6 1.3 constant_dynamic-update-slice_fusion.8
  38.9 1.3 constant_dynamic-update-slice_fusion.7
  40.2 1.3 constant_dynamic-update-slice_fusion.6
  41.5 1.3 constant_dynamic-update-slice_fusion.5
  42.8 1.3 constant_dynamic-update-slice_fusion.4
  44.1 1.3 constant_dynamic-update-slice_fusion.3
  45.4 1.3 constant_dynamic-update-slice_fusion.2
  46.7 1.3 constant_dynamic-update-slice_fusion.1
  48.0 7.3 %all-to-all-start.1 = ((bf16[32,32,128]{2,1,0:T(8,128)(2,1)}), bf16[32,32,128]{2,1,0:T(8,128)(2,1)S(1)}, u32[]{:S(2)}, u32[]{:S(2)}) async-start(bf16[32,32,128]{2,1,0:T(8,128)(2,1)} %constant_dynamic-update-slice_fusion.1), calls=%async_computation.1 | async-start | bytes 524288 | tf_op jit(solution)/shard_map/all_to_all | solution.py:59
  55.4 34.9 %negate_convert_fusion = (bf16[2048,1024]{1,0:T(8,128)(2,1)}, bf16[2048,1024]{1,0:T(8,128)(2,1)}) fusion(), kind=kLoop, calls=%fused_computation.13 | loop fusion | flops 35651584 | bytes 8388608 | tf_op jit(solution)/shard_map/convert.6
  91.3 4.4 %fusion.3 = f32[64,2048]{1,0:T(8,128)S(1)} fusion(bf16[2048,1024]{1,0:T(8,128)(2,1)} %get-tuple-element.13, bf16[2048,1024]{1,0:T(8,128)(2,1)} %get-tuple-element.14, f32[64,2048]{1,0:T(8,128)S(1)} %reshape.148, f32[2048]{0:T(1024)S(1)} %multiply_subtract_fusion, f32[64]{0:T(128)S(1)} %broadcast_multiply_fusion.1), kind=kOutput, calls=%fused_computation.9 | convolution fusion | flops 554041344 | bytes 9445632 | tf_op jit(solution)/shard_map/dot_general | solution.py:27
  99.7 15.2 %all-to-all-start = ((s32[16,1,16]{2,1,0:T(1,128)}), s32[16,1,16]{2,1,0:T(1,128)S(1)}, u32[]{:S(2)}, u32[]{:S(2)}) async-start(s32[16,1,16]{2,1,0:T(1,128)} %all_to_all.12), calls=%async_computation | async-start | bytes 16384 | tf_op jit(solution)/shard_map/all_to_all | solution.py:74
  115.0 11.0 %all-to-all-done = s32[16,1,16]{2,1,0:T(1,128)S(1)} async-done(((s32[16,1,16]{2,1,0:T(1,128)}), s32[16,1,16]{2,1,0:T(1,128)S(1)}, u32[]{:S(2)}, u32[]{:S(2)}) %all-to-all-start) | async-done | bytes 1056 | tf_op jit(solution)/shard_map/all_to_all | solution.py:74
  127.3 42.7 %all-gather.2.cloned.1.call-done = bf16[1024,4096]{1,0:T(8,128)(2,1)} async-done(((bf16[32,4096]{1,0:T(8,128)(2,1)}), bf16[1024,4096]{1,0:T(8,128)(2,1)}) %all-gather.2.cloned.1.call-update) | async-done | bytes 8388624 | tf_op jit(solution)/shard_map/all_gather | solution.py:77
  170.0 12.0 %gather_fusion = bf16[384,4096]{1,0:T(8,128)(2,1)S(1)} fusion(bf16[1024,4096]{1,0:T(8,128)(2,1)} %all-gather.2.cloned.1.call-done, s32[1024]{0:T(1024)S(1)} %pad_clamp_fusion.1), kind=kCustom, calls=%fused_computation | custom fusion | bytes 6292992 | tf_op jit(solution)/shard_map/jit(_take)/gather | solution.py:79
  182.5 1.7 copy-done
  184.1 1.5 slice.77
  185.6 12.7 %all-to-all-start.2 = ((bf16[16,16,4096]{2,1,0:T(8,128)(2,1)}), bf16[16,16,4096]{2,1,0:T(8,128)(2,1)S(1)}, u32[]{:S(2)}, u32[]{:S(2)}) async-start(bf16[16,16,4096]{2,1,0:T(8,128)(2,1)} %bitcast.82), calls=%async_computation.2 | async-start | bytes 4194304 | tf_op jit(solution)/shard_map/all_to_all | solution.py:83
  198.3 2.8 slice_convert_fusion
  201.1 4.0 %reshape.150 = f32[128,2,2,1024]{3,2,1,0:T(2,128)} reshape(f32[128,4096]{1,0:T(8,128)} %slice_convert_fusion) | data formatting | bytes 4194304 | tf_op jit(solution)/shard_map/reshape | solution.py:43
  205.2 87.5 %all-to-all-done.2 = bf16[16,16,4096]{2,1,0:T(8,128)(2,1)S(1)} async-done(((bf16[16,16,4096]{2,1,0:T(8,128)(2,1)}), bf16[16,16,4096]{2,1,0:T(8,128)(2,1)S(1)}, u32[]{:S(2)}, u32[]{:S(2)}) %all-to-all-start.2) | async-done | bytes 2097184 | tf_op jit(solution)/shard_map/all_to_all | solution.py:83
  293.8 1.6 gather.12
  295.4 2.2 fusion.10
  297.7 5.8 %add_reduce_fusion = (f32[128,1024]{1,0:T(8,128)S(1)}, f32[128,1024]{1,0:T(8,128)S(1)}) fusion(f32[128,2,2,1024]{3,2,1,0:T(2,128)S(1)} %fusion.10, f32[128,2,2,1024]{3,2,1,0:T(2,128)S(1)} %copy-done.1), kind=kLoop, calls=%fused_computation.23 | loop fusion | flops 1835008 | bytes 5242880 | tf_op jit(solution)/shard_map/reduce_sum | solution.py:45
  (46 shorter events, 8.8 us)
Async XLA Ops:
  48.0 42.4 %all-to-all-start.1 = ((bf16[32,32,128]{2,1,0:T(8,128)(2,1)}), bf16[32,32,128]{2,1,0:T(8,128)(2,1)S(1)}, u32[]{:S(2)}, u32[]{:S(2)}) async-start(bf16[32,32,128]{2,1,0:T(8,128)(2,1)} %constant_dynamic-update-slice_fusion.1), calls=%async_computation.1 | async-start | bytes 524288 | tf_op jit(solution)/shard_map/all_to_all | solution.py:59
  55.3 114.7 %all-gather.2.cloned.1.call-start = ((), (), s32[]{:S(2)}) async-start(), calls=%async_computation.3 | async-start | bytes 8650752 | tf_op jit(solution)/shard_map/all_gather | solution.py:77
  91.3 6.2 %copy-start.2 = (s32[128,1]{0,1:T(1,128)S(1)}, s32[128,1]{0,1:T(1,128)}, u32[]{:S(2)}) copy-start(s32[128,1]{0,1:T(1,128)} %param.6) | copy-start | bytes 1540
  91.3 23.6 %copy-start.3 = (s32[128]{0:T(128)S(1)}, s32[128]{0:T(128)}, u32[]{:S(2)}) copy-start(s32[128]{0:T(128)} %param.5) | copy-start | bytes 1540
  99.7 26.3 %all-to-all-start = ((s32[16,1,16]{2,1,0:T(1,128)}), s32[16,1,16]{2,1,0:T(1,128)S(1)}, u32[]{:S(2)}, u32[]{:S(2)}) async-start(s32[16,1,16]{2,1,0:T(1,128)} %all_to_all.12), calls=%async_computation | async-start | bytes 16384 | tf_op jit(solution)/shard_map/all_to_all | solution.py:74
  182.5 1.7 copy-start
  185.6 107.0 %all-to-all-start.2 = ((bf16[16,16,4096]{2,1,0:T(8,128)(2,1)}), bf16[16,16,4096]{2,1,0:T(8,128)(2,1)S(1)}, u32[]{:S(2)}, u32[]{:S(2)}) async-start(bf16[16,16,4096]{2,1,0:T(8,128)(2,1)} %bitcast.82), calls=%async_computation.2 | async-start | bytes 4194304 | tf_op jit(solution)/shard_map/all_to_all | solution.py:83
  293.8 3.8 %copy-start.1 = (f32[128,2,2,1024]{3,2,1,0:T(2,128)S(1)}, f32[128,2,2,1024]{3,2,1,0:T(2,128)}, u32[]{:S(2)}) copy-start(f32[128,2,2,1024]{3,2,1,0:T(2,128)} %reshape.150) | copy-start | bytes 6291460
Sparse Core Ops, SparseCore 0:
  97.6 72.3 all-gather.1
